TPU v7x, 32 devices: a whole 2x2x4 slice. The times are simulated.
32 devices in a mesh: grp: 2 (over y), mesh: 4 (over z), tm: 2 (over x), rep: 2 (over core).
Axes of the slice: x: 2, y: 2, z: 4, core: 2. Of those that a mesh axis runs over, the one named last changes fastest.
Arguments:
- right_side: float32 [4, 128, 64, 128], P(('grp', 'tm'), ('mesh', 'rep')), parts along dimension 0, may hold values from -25 to 25
- kappa_sq: float32 [256, 64], P(('grp', 'mesh', 'rep')), parts along dimension 0, may hold values from 0.25 to 4
- time_coupling: float32 [2], P('grp'), parts along dimension 0, may hold values from 0.15 to 0.45
- near_stiffness: float32 [128, 64, 384], P(('mesh', 'rep')), may hold values from -0.16 to 0.16, as said below
- far_stiffness: float32 [8, 64, 1536], P(('mesh', 'rep')), may hold values from -0.16 to 0.16, as said below
- near_columns: int32 [128, 6], P(('mesh', 'rep')), may hold values from 0 to 15, as said below
- face_blocks: int32 [8, 6, 4], P(('mesh', 'rep')), may hold values from 0 to 15, as said below
- face_counts: int32 [8, 6], P(('mesh', 'rep')), may hold values from 0 to 4, as said below
Outputs:
- solution_field: float32 [4, 128, 64, 128], P(('grp', 'tm'), ('mesh', 'rep')), parts along dimension 0
- residual: float32 [4, 128, 64, 128], P(('grp', 'tm'), ('mesh', 'rep')), parts along dimension 0
There are 2 independent parts, one for each index of `grp`. A program takes and returns all parts, laid end to end along the dimension named above; an argument that names none is the same for every part. Nothing has to cross between parts.
Inputs may be any that keep to these rules, and one draw needn't show every extreme that they name: face_counts[n(p, e), e'] = face_counts[p, e]; every partition sends 4 blocks toward at least one direction. `face_blocks`: the 4 blocks of one partition and direction are distinct. `near_columns`: for j < 3, slot 2j over the block rows of a partition is a permutation of its local blocks and slot 2j + 1 is the inverse permutation. `near_stiffness`: for j < 3, the block in slot 2j + 1 of block row b is the transpose of the block in slot 2j of the block row that slot 2j + 1 of b names. `far_stiffness`: G[n(p, e), e' * 4 + f] is the transpose of G[p, e * 4 + f].
All inputs are finite; a program needn't handle non-finite values.
Results may differ from a plain program's by a relative error of at most 0.00016.
Values sent between devices are 32-bit elements; how exact they have to be, the bound alone decides.
No kernel may reach another device: no remote copies, remote signals or barrier semaphores. Data moves between devices by JAX's collectives and lax.ppermute only.
A program may use at most 64 MiB of HBM per device.

v0:
```python
import jax
import jax.numpy as jnp
from jax import lax
from jax.sharding import PartitionSpec as P

ITERS = 2


def from_behind(block, axis, distance):
    devices = range(lax.axis_size(axis))
    route = [((i - distance) % len(devices), i) for i in devices]
    return lax.ppermute(block, axis, route)


def with_halo(value, sides, width):
    for axis, dim in sides:
        peers, length = (lax.axis_size(axis), value.shape[dim])
        up = [(i, (i + 1) % peers) for i in range(peers - 1)]
        down = [(j, i) for i, j in up]
        last = lax.slice_in_dim(value, length - width, length, axis=dim)
        initial = lax.slice_in_dim(value, 0, width, axis=dim)
        before = lax.ppermute(last, axis, up)
        after = lax.ppermute(initial, axis, down)
        value = jnp.concatenate([before, value, after], axis=dim)
    return value


def spatial(
    vector, kappa_sq, near_stiffness, far_stiffness, near_columns, face_blocks, face_counts
):
    hours_n, blocks_n, node_width, probes = vector.shape
    face_slots = face_blocks.shape[2]
    partitions = lax.axis_size(("mesh", "rep"))
    stride = partitions // 4 + 1
    offsets = (1, -1, 2, -2, stride, -stride)
    slot_blocks = face_blocks[0].reshape(-1)
    active = (jnp.arange(face_slots)[None, :] < face_counts[0][:, None]).astype(jnp.float32)
    outgoing = jnp.take(vector, slot_blocks, axis=1).reshape(
        hours_n, 6, face_slots, node_width, probes
    )
    outgoing = outgoing * active[None, :, :, None, None]
    arrived = []
    for heading in range(6):
        arrived.append(from_behind(outgoing[:, heading ^ 1], ("mesh", "rep"), -offsets[heading]))
    received = jnp.stack(arrived, axis=1).reshape(hours_n, 6 * face_slots, node_width, probes)
    nearby = jnp.take(vector, near_columns.reshape(-1), axis=1).reshape(
        hours_n, blocks_n, -1, probes
    )
    result = (3.0 + kappa_sq)[None, :, :, None] * vector
    result = result + jnp.einsum(
        "nik,hnkp->hnip",
        near_stiffness,
        nearby,
        precision=lax.Precision.HIGHEST,
        preferred_element_type=jnp.float32,
    )
    far_blocks = far_stiffness[0].reshape(node_width, 6 * face_slots, node_width)
    far_terms = jnp.einsum(
        "iqk,hqkp->hqip",
        far_blocks,
        received,
        precision=lax.Precision.HIGHEST,
        preferred_element_type=jnp.float32,
    )
    landing = (slot_blocks[None, :] == jnp.arange(blocks_n)[:, None]).astype(jnp.float32)
    result = result + jnp.einsum(
        "nq,hqip->hnip",
        landing,
        far_terms,
        precision=lax.Precision.HIGHEST,
        preferred_element_type=jnp.float32,
    )
    return result


def operate(
    vector,
    kappa_sq,
    time_coupling,
    near_stiffness,
    far_stiffness,
    near_columns,
    face_blocks,
    face_counts,
):
    product = spatial(
        vector, kappa_sq, near_stiffness, far_stiffness, near_columns, face_blocks, face_counts
    )
    padded = with_halo(product, (("tm", 0),), 1)
    return product - time_coupling[0] * (padded[:-2] + padded[2:])


def two_products(residual, applied):
    return lax.psum(
        (jnp.sum(residual * residual, axis=(0, 1, 2)), jnp.sum(residual * applied, axis=(0, 1, 2))),
        ("mesh", "tm", "rep"),
    )


def shards(
    right_side,
    kappa_sq,
    time_coupling,
    near_stiffness,
    far_stiffness,
    near_columns,
    face_blocks,
    face_counts,
):

    def apply_operator(vector):
        return operate(
            vector,
            kappa_sq,
            time_coupling,
            near_stiffness,
            far_stiffness,
            near_columns,
            face_blocks,
            face_counts,
        )

    solution_field = jnp.zeros_like(right_side)
    residual = right_side
    applied = apply_operator(residual)
    norm_now, product = two_products(residual, applied)
    step_size = norm_now / product
    direction = residual
    applied_dir = applied
    for iteration in range(ITERS):
        solution_field = solution_field + step_size * direction
        residual = residual - step_size * applied_dir
        if iteration + 1 < ITERS:
            applied = apply_operator(residual)
            norm_next, product = two_products(residual, applied)
            beta_ratio = norm_next / norm_now
            step_size = norm_next / (product - beta_ratio * norm_next / step_size)
            direction = residual + beta_ratio * direction
            applied_dir = applied + beta_ratio * applied_dir
            norm_now = norm_next
    return (solution_field, residual)


def solution(mesh):
    placed = (
        P(("grp", "tm"), ("mesh", "rep"), None, None),
        P(("grp", "mesh", "rep"), None),
        P("grp"),
        P(("mesh", "rep"), None, None),
        P(("mesh", "rep"), None, None),
        P(("mesh", "rep"), None),
        P(("mesh", "rep"), None, None),
        P(("mesh", "rep"), None),
    )
    return jax.shard_map(
        shards,
        mesh=mesh,
        in_specs=placed,
        out_specs=(
            P(("grp", "tm"), ("mesh", "rep"), None, None),
            P(("grp", "tm"), ("mesh", "rep"), None, None),
        ),
        check_vma=False,
    )
```

profile of v0, /device:TPU:0, one launch (start us, length us, event | category | flops | bytes accessed | tf_op | source)
XLA Modules:
  0.0 164.5 jit_solution(14381647301428617906)
XLA Ops:
  0.6 0.0 copy-start
  0.6 0.9 copy.19
  1.5 0.1 reshape_squeeze.8
  1.6 0.5 copy-done.8
  2.1 0.7 fusion.15
  2.9 0.8 copy.18
  3.6 0.1 reshape.135
  3.7 0.0 copy-start.4
  3.8 1.7 %gather_fusion.1 = f32[24,64,128]{2,1,0:T(8,128)S(1)} fusion(f32[16,64,128]{2,1,0:T(8,128)} %bitcast.116, s32[1024]{0:T(1024)S(1)} %get-tuple-element.30), kind=kCustom, calls=%fused_computation.1.clone | custom fusion | bytes 1572960 | tf_op jit(solution)/shard_map/jit(_take)/gather | solution.py:38
  5.5 0.0 copy-start.1
  5.5 0.1 bitcast_select_fusion.3
  5.6 0.1 broadcast_multiply_fusion.1
  5.7 0.8 slice_bitcast_fusion.6
  6.5 2.5 %collective-permute-start.5 = (f32[1,4,64,128]{3,2,1,0:T(8,128)S(1)}, f32[1,4,64,128]{3,2,1,0:T(8,128)}, u32[]{:S(2)}, u32[]{:S(2)}) collective-permute-start(f32[1,4,64,128]{3,2,1,0:T(8,128)S(1)} %get-tuple-element.22), channel_id=1, source_target_pairs={{9,0},{12,1},{13,4},{0,5},{1,8},{4,9},{5,12},{8,13},{11,2},{14,3},... | collective-permute-start | bytes 393224 | tf_op jit(solution)/shard_map/ppermute | solution.py:12
  9.0 1.0 collective-permute-start.4
  10.0 2.2 %collective-permute-start.3 = (f32[1,4,64,128]{3,2,1,0:T(8,128)}, f32[1,4,64,128]{3,2,1,0:T(8,128)}, u32[]{:S(2)}, u32[]{:S(2)}) collective-permute-start(f32[1,4,64,128]{3,2,1,0:T(8,128)} %get-tuple-element.24), channel_id=1, source_target_pairs={{12,0},{13,1},{0,4},{1,5},{4,8},{5,9},{8,12},{9,13},{14,2},{15,3},... | collective-permute-start | bytes 393224 | tf_op jit(solution)/shard_map/ppermute | solution.py:12
  12.2 2.0 %collective-permute-start.2 = (f32[1,4,64,128]{3,2,1,0:T(8,128)}, f32[1,4,64,128]{3,2,1,0:T(8,128)}, u32[]{:S(2)}, u32[]{:S(2)}) collective-permute-start(f32[1,4,64,128]{3,2,1,0:T(8,128)} %get-tuple-element.25), channel_id=1, source_target_pairs={{4,0},{5,1},{8,4},{9,5},{12,8},{13,9},{0,12},{1,13},{6,2},{7,3},{1... | collective-permute-start | bytes 393224 | tf_op jit(solution)/shard_map/ppermute | solution.py:12
  14.2 0.7 collective-permute-start
  14.9 0.2 reshape_squeeze.9
  15.1 2.4 %gather_fusion = f32[96,64,128]{2,1,0:T(8,128)} fusion(f32[16,64,128]{2,1,0:T(8,128)S(1)} %bitcast.117, s32[1024]{0:T(1024)S(1)} %get-tuple-element.31), kind=kCustom, calls=%fused_computation.clone | custom fusion | bytes 6291840 | tf_op jit(solution)/shard_map/jit(_take)/gather | solution.py:46
  17.5 2.2 %bitcast_select_fusion.1 = f32[1,96,64,128]{3,2,1,0:T(8,128)S(1)} fusion(f32[96,64,128]{2,1,0:T(8,128)} %gather_fusion, pred[96]{0:T(512)(128)(4,1)S(1)} %compare_and_fusion.1), kind=kLoop, calls=%fused_computation.5 | loop fusion | flops 786432 | bytes 6291552 | tf_op jit(solution)/shard_map/jit(_take)/select_n | solution.py:46
  19.7 3.2 %collective-permute-done = f32[1,4,64,128]{3,2,1,0:T(8,128)} collective-permute-done((f32[1,4,64,128]{3,2,1,0:T(8,128)}, f32[1,4,64,128]{3,2,1,0:T(8,128)}, u32[]{:S(2)}, u32[]{:S(2)}) %collective-permute-start) | collective-permute-done | bytes 131104 | tf_op jit(solution)/shard_map/ppermute | solution.py:12
  22.9 1.4 collective-permute-start.1
  24.3 0.9 bitcast_dynamic-update-slice_fusion.11
  25.2 4.2 %collective-permute-done.1 = f32[1,4,64,128]{3,2,1,0:T(8,128)S(1)} collective-permute-done((f32[1,4,64,128]{3,2,1,0:T(8,128)S(1)}, f32[1,4,64,128]{3,2,1,0:T(8,128)S(1)}, u32[]{:S(2)}, u32[]{:S(2)}) %collective-permute-start.1) | collective-permute-done | bytes 131104 | tf_op jit(solution)/shard_map/ppermute | solution.py:12
  29.4 0.9 bitcast_dynamic-update-slice_fusion.9
  30.3 0.0 collective-permute-done.3
  30.3 0.9 bitcast_dynamic-update-slice_fusion.8
  31.3 0.0 collective-permute-done.4
  31.3 0.9 bitcast_dynamic-update-slice_fusion.7
  32.2 0.9 bitcast_dynamic-update-slice_fusion.6
  33.1 0.9 convolution_bitcast_fusion.1
  34.1 0.9 fusion.6
  34.9 2.6 %fusion.1 = f32[1,16,64,128]{3,2,1,0:T(8,128)S(1)} fusion(f32[16,384,128]{2,1,0:T(8,128)S(1)} %bitcast.121, f32[16,64,384]{2,1,0:T(8,128)S(1)} %copy-done, f32[64,128,16]{1,2,0:T(8,128)S(1)} %fusion.6, f32[1,16,64,128]{3,2,1,0:T(8,128)S(1)} %copy-done.1, f32[16,64]{1,0:T(8,128)S(1)} %broadcast_add_fusion), kind=kOutput, calls=%fused_computation.11 | convolution fusion | flops 604372992 | bytes 6295552 | tf_op jit(solution)/shard_map/nik,hnkp->hnip/dot_general | solution.py:50
  37.5 1.3 collective-permute-start.7
  38.8 4.6 %collective-permute-start.6 = (f32[1,16,64,128]{3,2,1,0:T(8,128)S(1)}, f32[1,16,64,128]{3,2,1,0:T(8,128)S(1)}, u32[]{:S(2)}, u32[]{:S(2)}) collective-permute-start(f32[1,16,64,128]{3,2,1,0:T(8,128)S(1)} %fusion.1), channel_id=1, source_target_pairs={{0,2},{1,3},{4,6},{5,7},{8,10},{9,11},{12,14},{13,15},{16,18},{17,... | collective-permute-start | bytes 1572872 | tf_op jit(solution)/shard_map/ppermute | solution.py:22
  44.1 6.0 %collective-permute-done.7 = f32[1,16,64,128]{3,2,1,0:T(8,128)S(1)} collective-permute-done((f32[1,16,64,128]{3,2,1,0:T(8,128)S(1)}, f32[1,16,64,128]{3,2,1,0:T(8,128)S(1)}, u32[]{:S(2)}, u32[]{:S(2)}) %collective-permute-start.7) | collective-permute-done | bytes 524320 | tf_op jit(solution)/shard_map/ppermute | solution.py:23
  50.1 1.2 collective-permute-done.6
  51.3 1.0 multiply_reduce_fusion.2
  52.3 32.0 %all-reduce.1 = (f32[128]{0:T(128)S(1)}, f32[128]{0:T(128)S(1)}) all-reduce(f32[128]{0:T(128)S(1)} %get-tuple-element.7, f32[128]{0:T(128)S(1)} %get-tuple-element.6), channel_id=1, replica_groups=mesh['grp'=2,'mesh'=4,'tm'=2,'rep'=2] {'mesh','tm','rep'}, use_global_device_ids=true, to_apply=%region_1.2 | all-reduce | flops 256 | bytes 2048 | tf_op jit(solution)/shard_map/psum | solution.py:94
  84.2 1.1 multiply_subtract_fusion.2
  85.3 1.6 gather_fusion.3
  87.0 2.4 %gather_fusion.2 = f32[96,64,128]{2,1,0:T(8,128)} fusion(f32[16,64,128]{2,1,0:T(8,128)S(1)} %bitcast.119, s32[1024]{0:T(1024)S(1)} %get-tuple-element.31), kind=kCustom, calls=%fused_computation.2.clone | custom fusion | bytes 6291840 | tf_op jit(solution)/shard_map/jit(_take)/gather | solution.py:46
  89.4 1.4 bitcast_select_fusion.2
  90.8 0.1 broadcast_multiply_fusion
  90.9 0.1 slice_bitcast_fusion
  91.0 0.1 collective-permute-start.13
  91.0 2.6 %collective-permute-start.12 = (f32[1,4,64,128]{3,2,1,0:T(8,128)S(1)}, f32[1,4,64,128]{3,2,1,0:T(8,128)S(1)}, u32[]{:S(2)}, u32[]{:S(2)}) collective-permute-start(f32[1,4,64,128]{3,2,1,0:T(8,128)S(1)} %get-tuple-element.17), channel_id=1, source_target_pairs={{5,0},{8,1},{9,4},{12,5},{13,8},{0,9},{1,12},{4,13},{7,2},{10,3},{... | collective-permute-start | bytes 393224 | tf_op jit(solution)/shard_map/ppermute | solution.py:12
  93.7 3.8 %collective-permute-start.10 = (f32[1,4,64,128]{3,2,1,0:T(8,128)S(1)}, f32[1,4,64,128]{3,2,1,0:T(8,128)S(1)}, u32[]{:S(2)}, u32[]{:S(2)}) collective-permute-start(f32[1,4,64,128]{3,2,1,0:T(8,128)S(1)} %get-tuple-element.19), channel_id=1, source_target_pairs={{4,0},{5,1},{8,4},{9,5},{12,8},{13,9},{0,12},{1,13},{6,2},{7,3},{1... | collective-permute-start | bytes 393224 | tf_op jit(solution)/shard_map/ppermute | solution.py:12
  97.5 0.3 bitcast_select_fusion
  97.8 5.5 %collective-permute-done.8 = f32[1,4,64,128]{3,2,1,0:T(8,128)S(1)} collective-permute-done((f32[1,4,64,128]{3,2,1,0:T(8,128)S(1)}, f32[1,4,64,128]{3,2,1,0:T(8,128)S(1)}, u32[]{:S(2)}, u32[]{:S(2)}) %collective-permute-start.8) | collective-permute-done | bytes 131104 | tf_op jit(solution)/shard_map/ppermute | solution.py:12
  103.3 2.1 %collective-permute-start.9 = (f32[1,4,64,128]{3,2,1,0:T(8,128)S(1)}, f32[1,4,64,128]{3,2,1,0:T(8,128)S(1)}, u32[]{:S(2)}, u32[]{:S(2)}) collective-permute-start(f32[1,4,64,128]{3,2,1,0:T(8,128)S(1)} %get-tuple-element.20), channel_id=1, source_target_pairs={{13,0},{0,1},{1,4},{4,5},{5,8},{8,9},{9,12},{12,13},{15,2},{2,3},{... | collective-permute-start | bytes 393224 | tf_op jit(solution)/shard_map/ppermute | solution.py:12
  105.5 4.3 %collective-permute-done.9 = f32[1,4,64,128]{3,2,1,0:T(8,128)S(1)} collective-permute-done((f32[1,4,64,128]{3,2,1,0:T(8,128)S(1)}, f32[1,4,64,128]{3,2,1,0:T(8,128)S(1)}, u32[]{:S(2)}, u32[]{:S(2)}) %collective-permute-start.9) | collective-permute-done | bytes 131104 | tf_op jit(solution)/shard_map/ppermute | solution.py:12
  109.9 0.9 convolution_bitcast_fusion
  110.9 0.9 fusion.4
  111.7 0.0 copy-start.3
  111.8 2.6 %fusion.3 = f32[1,16,64,128]{3,2,1,0:T(8,128)S(1)} fusion(f32[16,384,128]{2,1,0:T(8,128)S(1)} %bitcast.120, f32[16,64,384]{2,1,0:T(8,128)S(1)} %copy-done, f32[64,128,16]{1,2,0:T(8,128)S(1)} %fusion.4, f32[1,16,64,128]{3,2,1,0:T(8,128)S(1)} %multiply_subtract_fusion.2, f32[16,64]{1,0:T(8,128)S(1)} %broadcast_add_fusion), kind=kOutput, calls=%fused_computation.13 | convolution fusion | flops 604372992 | bytes 6295552 | tf_op jit(solution)/shard_map/nik,hnkp->hnip/dot_general | solution.py:50
  114.4 1.3 collective-permute-start.15
  115.7 4.6 %collective-permute-start.14 = (f32[1,16,64,128]{3,2,1,0:T(8,128)S(1)}, f32[1,16,64,128]{3,2,1,0:T(8,128)S(1)}, u32[]{:S(2)}, u32[]{:S(2)}) collective-permute-start(f32[1,16,64,128]{3,2,1,0:T(8,128)S(1)} %fusion.3), channel_id=1, source_target_pairs={{0,2},{1,3},{4,6},{5,7},{8,10},{9,11},{12,14},{13,15},{16,18},{17,... | collective-permute-start | bytes 1572872 | tf_op jit(solution)/shard_map/ppermute | solution.py:22
  120.3 7.4 %collective-permute-done.15 = f32[1,16,64,128]{3,2,1,0:T(8,128)S(1)} collective-permute-done((f32[1,16,64,128]{3,2,1,0:T(8,128)S(1)}, f32[1,16,64,128]{3,2,1,0:T(8,128)S(1)}, u32[]{:S(2)}, u32[]{:S(2)}) %collective-permute-start.15) | collective-permute-done | bytes 524320 | tf_op jit(solution)/shard_map/ppermute | solution.py:23
  127.7 1.2 collective-permute-done.14
  128.9 1.0 multiply_reduce_fusion
  129.9 32.4 %all-reduce = (f32[128]{0:T(128)S(1)}, f32[128]{0:T(128)S(1)}) all-reduce(f32[128]{0:T(128)S(1)} %get-tuple-element.5, f32[128]{0:T(128)S(1)} %get-tuple-element.4), channel_id=1, replica_groups=mesh['grp'=2,'mesh'=4,'tm'=2,'rep'=2] {'mesh','tm','rep'}, use_global_device_ids=true, to_apply=%region_5.8 | all-reduce | flops 256 | bytes 2048 | tf_op jit(solution)/shard_map/psum | solution.py:94
  162.3 2.2 %multiply_subtract_fusion = (f32[1,16,64,128]{3,2,1,0:T(8,128)}, f32[1,16,64,128]{3,2,1,0:T(8,128)}) fusion(f32[1,16,64,128]{3,2,1,0:T(8,128)S(1)} %multiply_subtract_fusion.2, f32[1,16,64,128]{3,2,1,0:T(8,128)} %get-tuple-element.14, f32[1,16,64,128]{3,2,1,0:T(8,128)S(1)} %copy-done.3, f32[128]{0:T(128)S(1)} %get-tuple-element.13, ...), kind=kLoop, calls=%fused_computation.22 | loop fusion | flops 1179648 | bytes 3147264 | tf_op jit(solution)/shard_map/sub | solution.py:132
  (48 shorter events, 0.2 us)
Async XLA Ops:
  0.6 34.3 %copy-start = (f32[16,64,384]{2,1,0:T(8,128)S(1)}, f32[16,64,384]{2,1,0:T(8,128)}, u32[]{:S(2)}) copy-start(f32[16,64,384]{2,1,0:T(8,128)} %param.15) | copy-start | bytes 4718596
  1.6 0.5 copy-start.8
  1.6 4.0 %copy-start.11 = (pred[24]{0:T(512)(128)(4,1)}, pred[24]{0:T(512)(128)(4,1)S(1)}, u32[]{:S(2)}) copy-start(pred[24]{0:T(512)(128)(4,1)S(1)} %compare_and_fusion) | copy-start | bytes 76
  3.7 1.9 %copy-start.7 = (s32[1024]{0:T(1024)}, s32[1024]{0:T(1024)S(1)}, u32[]{:S(2)}) copy-start(s32[1024]{0:T(1024)S(1)} %get-tuple-element.30) | copy-start | bytes 12292
  3.7 11.2 %copy-start.4 = (f32[1,64,1536]{2,1,0:T(8,128)S(1)}, f32[1,64,1536]{2,1,0:T(8,128)}, u32[]{:S(2)}) copy-start(f32[1,64,1536]{2,1,0:T(8,128)} %param.16) | copy-start | bytes 1179652
  5.5 9.6 %copy-start.1 = (f32[1,16,64,128]{3,2,1,0:T(8,128)S(1)}, f32[1,16,64,128]{3,2,1,0:T(8,128)}, u32[]{:S(2)}) copy-start(f32[1,16,64,128]{3,2,1,0:T(8,128)} %param.12) | copy-start | bytes 1572868
  6.5 25.7 %collective-permute-start.5 = (f32[1,4,64,128]{3,2,1,0:T(8,128)S(1)}, f32[1,4,64,128]{3,2,1,0:T(8,128)}, u32[]{:S(2)}, u32[]{:S(2)}) collective-permute-start(f32[1,4,64,128]{3,2,1,0:T(8,128)S(1)} %get-tuple-element.22), channel_id=1, source_target_pairs={{9,0},{12,1},{13,4},{0,5},{1,8},{4,9},{5,12},{8,13},{11,2},{14,3},... | collective-permute-start | bytes 393224 | tf_op jit(solution)/shard_map/ppermute | solution.py:12
  9.0 22.3 %collective-permute-start.4 = (f32[1,4,64,128]{3,2,1,0:T(8,128)S(1)}, f32[1,4,64,128]{3,2,1,0:T(8,128)}, u32[]{:S(2)}, u32[]{:S(2)}) collective-permute-start(f32[1,4,64,128]{3,2,1,0:T(8,128)S(1)} %get-tuple-element.23), channel_id=1, source_target_pairs={{5,0},{8,1},{9,4},{12,5},{13,8},{0,9},{1,12},{4,13},{7,2},{10,3},{... | collective-permute-start | bytes 393224 | tf_op jit(solution)/shard_map/ppermute | solution.py:12
  10.0 20.3 %collective-permute-start.3 = (f32[1,4,64,128]{3,2,1,0:T(8,128)}, f32[1,4,64,128]{3,2,1,0:T(8,128)}, u32[]{:S(2)}, u32[]{:S(2)}) collective-permute-start(f32[1,4,64,128]{3,2,1,0:T(8,128)} %get-tuple-element.24), channel_id=1, source_target_pairs={{12,0},{13,1},{0,4},{1,5},{4,8},{5,9},{8,12},{9,13},{14,2},{15,3},... | collective-permute-start | bytes 393224 | tf_op jit(solution)/shard_map/ppermute | solution.py:12
  12.2 17.2 %collective-permute-start.2 = (f32[1,4,64,128]{3,2,1,0:T(8,128)}, f32[1,4,64,128]{3,2,1,0:T(8,128)}, u32[]{:S(2)}, u32[]{:S(2)}) collective-permute-start(f32[1,4,64,128]{3,2,1,0:T(8,128)} %get-tuple-element.25), channel_id=1, source_target_pairs={{4,0},{5,1},{8,4},{9,5},{12,8},{13,9},{0,12},{1,13},{6,2},{7,3},{1... | collective-permute-start | bytes 393224 | tf_op jit(solution)/shard_map/ppermute | solution.py:12
  14.2 8.7 %collective-permute-start = (f32[1,4,64,128]{3,2,1,0:T(8,128)}, f32[1,4,64,128]{3,2,1,0:T(8,128)}, u32[]{:S(2)}, u32[]{:S(2)}) collective-permute-start(f32[1,4,64,128]{3,2,1,0:T(8,128)} %get-tuple-element.27), channel_id=1, source_target_pairs={{1,0},{4,1},{5,4},{8,5},{9,8},{12,9},{13,12},{0,13},{3,2},{6,3},{7... | collective-permute-start | bytes 393224 | tf_op jit(solution)/shard_map/ppermute | solution.py:12
  14.9 2.6 %copy-start.13 = (pred[96]{0:T(512)(128)(4,1)}, pred[96]{0:T(512)(128)(4,1)S(1)}, u32[]{:S(2)}) copy-start(pred[96]{0:T(512)(128)(4,1)S(1)} %compare_and_fusion.1) | copy-start | bytes 292
  17.5 2.2 %copy-start.6 = (f32[16,64]{1,0:T(8,128)S(1)}, f32[16,64]{1,0:T(8,128)}, u32[]{:S(2)}) copy-start(f32[16,64]{1,0:T(8,128)} %param.13) | copy-start | bytes 12292
  17.5 5.4 %copy-start.5 = (f32[1,4,64,128]{3,2,1,0:T(8,128)S(1)}, f32[1,4,64,128]{3,2,1,0:T(8,128)}, u32[]{:S(2)}) copy-start(f32[1,4,64,128]{3,2,1,0:T(8,128)} %get-tuple-element.26) | copy-start | bytes 393220
  19.7 14.3 %copy-start.9 = (s32[24]{0:T(128)S(1)}, s32[24]{0:T(128)}, u32[]{:S(2)}) copy-start(s32[24]{0:T(128)} %copy-done.8) | copy-start | bytes 292
  22.9 6.5 %collective-permute-start.1 = (f32[1,4,64,128]{3,2,1,0:T(8,128)S(1)}, f32[1,4,64,128]{3,2,1,0:T(8,128)S(1)}, u32[]{:S(2)}, u32[]{:S(2)}) collective-permute-start(f32[1,4,64,128]{3,2,1,0:T(8,128)S(1)} %copy-done.5), channel_id=1, source_target_pairs={{13,0},{0,1},{1,4},{4,5},{5,8},{8,9},{9,12},{12,13},{15,2},{2,3},{... | collective-permute-start | bytes 393224 | tf_op jit(solution)/shard_map/ppermute | solution.py:12
  37.5 12.6 %collective-permute-start.7 = (f32[1,16,64,128]{3,2,1,0:T(8,128)S(1)}, f32[1,16,64,128]{3,2,1,0:T(8,128)S(1)}, u32[]{:S(2)}, u32[]{:S(2)}) collective-permute-start(f32[1,16,64,128]{3,2,1,0:T(8,128)S(1)} %fusion.1), channel_id=1, source_target_pairs={{2,0},{3,1},{6,4},{7,5},{10,8},{11,9},{14,12},{15,13},{18,16},{19,... | collective-permute-start | bytes 1572872 | tf_op jit(solution)/shard_map/ppermute | solution.py:23
  38.8 12.5 %collective-permute-start.6 = (f32[1,16,64,128]{3,2,1,0:T(8,128)S(1)}, f32[1,16,64,128]{3,2,1,0:T(8,128)S(1)}, u32[]{:S(2)}, u32[]{:S(2)}) collective-permute-start(f32[1,16,64,128]{3,2,1,0:T(8,128)S(1)} %fusion.1), channel_id=1, source_target_pairs={{0,2},{1,3},{4,6},{5,7},{8,10},{9,11},{12,14},{13,15},{16,18},{17,... | collective-permute-start | bytes 1572872 | tf_op jit(solution)/shard_map/ppermute | solution.py:22
  87.0 2.4 %copy-start.12 = (pred[24]{0:T(512)(128)(4,1)S(1)}, pred[24]{0:T(512)(128)(4,1)}, u32[]{:S(2)}) copy-start(pred[24]{0:T(512)(128)(4,1)} %copy-done.11) | copy-start | bytes 76
  89.4 8.1 %copy-start.2 = (f32[96,64,128]{2,1,0:T(8,128)S(1)}, f32[96,64,128]{2,1,0:T(8,128)}, u32[]{:S(2)}) copy-start(f32[96,64,128]{2,1,0:T(8,128)} %gather_fusion.2) | copy-start | bytes 9437188
  89.4 8.1 %copy-start.14 = (pred[96]{0:T(512)(128)(4,1)S(1)}, pred[96]{0:T(512)(128)(4,1)}, u32[]{:S(2)}) copy-start(pred[96]{0:T(512)(128)(4,1)} %copy-done.13) | copy-start | bytes 292
  91.0 18.9 %collective-permute-start.13 = (f32[1,4,64,128]{3,2,1,0:T(8,128)S(1)}, f32[1,4,64,128]{3,2,1,0:T(8,128)S(1)}, u32[]{:S(2)}, u32[]{:S(2)}) collective-permute-start(f32[1,4,64,128]{3,2,1,0:T(8,128)S(1)} %get-tuple-element.16), channel_id=1, source_target_pairs={{9,0},{12,1},{13,4},{0,5},{1,8},{4,9},{5,12},{8,13},{11,2},{14,3},... | collective-permute-start | bytes 393224 | tf_op jit(solution)/shard_map/ppermute | solution.py:12
  91.0 18.8 %collective-permute-start.12 = (f32[1,4,64,128]{3,2,1,0:T(8,128)S(1)}, f32[1,4,64,128]{3,2,1,0:T(8,128)S(1)}, u32[]{:S(2)}, u32[]{:S(2)}) collective-permute-start(f32[1,4,64,128]{3,2,1,0:T(8,128)S(1)} %get-tuple-element.17), channel_id=1, source_target_pairs={{5,0},{8,1},{9,4},{12,5},{13,8},{0,9},{1,12},{4,13},{7,2},{10,3},{... | collective-permute-start | bytes 393224 | tf_op jit(solution)/shard_map/ppermute | solution.py:12
  93.7 16.2 %collective-permute-start.11 = (f32[1,4,64,128]{3,2,1,0:T(8,128)S(1)}, f32[1,4,64,128]{3,2,1,0:T(8,128)S(1)}, u32[]{:S(2)}, u32[]{:S(2)}) collective-permute-start(f32[1,4,64,128]{3,2,1,0:T(8,128)S(1)} %get-tuple-element.18), channel_id=1, source_target_pairs={{12,0},{13,1},{0,4},{1,5},{4,8},{5,9},{8,12},{9,13},{14,2},{15,3},... | collective-permute-start | bytes 393224 | tf_op jit(solution)/shard_map/ppermute | solution.py:12
  93.7 16.2 %collective-permute-start.10 = (f32[1,4,64,128]{3,2,1,0:T(8,128)S(1)}, f32[1,4,64,128]{3,2,1,0:T(8,128)S(1)}, u32[]{:S(2)}, u32[]{:S(2)}) collective-permute-start(f32[1,4,64,128]{3,2,1,0:T(8,128)S(1)} %get-tuple-element.19), channel_id=1, source_target_pairs={{4,0},{5,1},{8,4},{9,5},{12,8},{13,9},{0,12},{1,13},{6,2},{7,3},{1... | collective-permute-start | bytes 393224 | tf_op jit(solution)/shard_map/ppermute | solution.py:12
  97.5 5.9 %collective-permute-start.8 = (f32[1,4,64,128]{3,2,1,0:T(8,128)S(1)}, f32[1,4,64,128]{3,2,1,0:T(8,128)S(1)}, u32[]{:S(2)}, u32[]{:S(2)}) collective-permute-start(f32[1,4,64,128]{3,2,1,0:T(8,128)S(1)} %get-tuple-element.21), channel_id=1, source_target_pairs={{1,0},{4,1},{5,4},{8,5},{9,8},{12,9},{13,12},{0,13},{3,2},{6,3},{7... | collective-permute-start | bytes 393224 | tf_op jit(solution)/shard_map/ppermute | solution.py:12
  97.8 13.1 %copy-start.10 = (s32[24]{0:T(128)S(1)}, s32[24]{0:T(128)}, u32[]{:S(2)}) copy-start(s32[24]{0:T(128)} %copy-done.8) | copy-start | bytes 292
  103.3 6.5 %collective-permute-start.9 = (f32[1,4,64,128]{3,2,1,0:T(8,128)S(1)}, f32[1,4,64,128]{3,2,1,0:T(8,128)S(1)}, u32[]{:S(2)}, u32[]{:S(2)}) collective-permute-start(f32[1,4,64,128]{3,2,1,0:T(8,128)S(1)} %get-tuple-element.20), channel_id=1, source_target_pairs={{13,0},{0,1},{1,4},{4,5},{5,8},{8,9},{9,12},{12,13},{15,2},{2,3},{... | collective-permute-start | bytes 393224 | tf_op jit(solution)/shard_map/ppermute | solution.py:12
  111.7 50.6 %copy-start.3 = (f32[1,16,64,128]{3,2,1,0:T(8,128)S(1)}, f32[1,16,64,128]{3,2,1,0:T(8,128)}, u32[]{:S(2)}) copy-start(f32[1,16,64,128]{3,2,1,0:T(8,128)} %get-tuple-element.15) | copy-start | bytes 1572868
  114.4 13.3 %collective-permute-start.15 = (f32[1,16,64,128]{3,2,1,0:T(8,128)S(1)}, f32[1,16,64,128]{3,2,1,0:T(8,128)S(1)}, u32[]{:S(2)}, u32[]{:S(2)}) collective-permute-start(f32[1,16,64,128]{3,2,1,0:T(8,128)S(1)} %fusion.3), channel_id=1, source_target_pairs={{2,0},{3,1},{6,4},{7,5},{10,8},{11,9},{14,12},{15,13},{18,16},{19,... | collective-permute-start | bytes 1572872 | tf_op jit(solution)/shard_map/ppermute | solution.py:23
  115.7 13.2 %collective-permute-start.14 = (f32[1,16,64,128]{3,2,1,0:T(8,128)S(1)}, f32[1,16,64,128]{3,2,1,0:T(8,128)S(1)}, u32[]{:S(2)}, u32[]{:S(2)}) collective-permute-start(f32[1,16,64,128]{3,2,1,0:T(8,128)S(1)} %fusion.3), channel_id=1, source_target_pairs={{0,2},{1,3},{4,6},{5,7},{8,10},{9,11},{12,14},{13,15},{16,18},{17,... | collective-permute-start | bytes 1572872 | tf_op jit(solution)/shard_map/ppermute | solution.py:22
where the time goes:
time: 165 us
  blocking collectives  64.4 us (39%)
  waiting for transfers between devices  33.1 us (20%)
  starting transfers between devices  30.1 us (18%)
  local copies, waits for them, and re-layouts  16.1 us (10%)
  other arithmetic  10.3 us (6%)
  matrix products  8.76 us (5%)
  between operations  1.73 us (1%)
    psum x2, blocking collectives, two_products(): lax.psum((jnp.sum(residual * residual, axis=(0, 1, 2)), jnp.sum(residual...  64.4 us
    ppermute x12, starting transfers between devices, from_behind(): return lax.ppermute(block, axis, route)  18.3 us
    ppermute x12, waiting for transfers between devices, from_behind(): return lax.ppermute(block, axis, route)  17.3 us
    ppermute x2, waiting for transfers between devices, with_halo(): after = lax.ppermute(initial, axis, down)  13.4 us
    ppermute x2, starting transfers between devices, with_halo(): before = lax.ppermute(last, axis, up)  9.21 us
    unnamed x42, local copies, waits for them, and re-layouts  5.93 us
    dot_general x2, matrix products, spatial(): jnp.einsum('nik,hnkp->hnip', near_stiffness, nearby, precision=lax.Precis...  5.2 us
    gather x2, local copies, waits for them, and re-layouts, spatial(): jnp.take(vector, near_columns.reshape(-1), axis=1)  4.79 us
  transfers between devices with their start and end apart: 16, of which 8 were waited for; matrix products, arithmetic and copies ran while one was open for 5% of the time, Pallas kernels for 0%

commit v1 on v0

--- a/solution.py
+++ b/solution.py
@@ -92,8 +92,14 @@
 
 def two_products(residual, applied):
     return lax.psum(
-        (jnp.sum(residual * residual, axis=(0, 1, 2)), jnp.sum(residual * applied, axis=(0, 1, 2))),
-        ("mesh", "tm", "rep"),
+        lax.psum(
+            (
+                jnp.sum(residual * residual, axis=(0, 1, 2)),
+                jnp.sum(residual * applied, axis=(0, 1, 2)),
+            ),
+            ("tm", "rep"),
+        ),
+        "mesh",
     )
 
 

time: 165 us -> 138 us (0.84)
  blocking collectives: 64.4 us -> 37.3 us
    psum x2, blocking collectives: 64.4 us -> 12 us  [two_products(): lax.psum((jnp.sum(residual * residual, axis=(0, 1, 2)), jnp.sum(residual...]
    psum x0 -> x2, blocking collectives: none -> 25.3 us  [two_products(): lax.psum(lax.psum((jnp.sum(residual * residual, axis=(0, 1, 2)), jnp.sum(...]
  transfers between devices with their start and end apart: 16 -> 16, of which waited for: 8 -> 8; matrix products, arithmetic and copies ran while one was open for 5% -> 6% of each run, Pallas kernels for 0% -> 0%
where the time goes in v1:
time: 138 us
  blocking collectives  37.3 us (27%)
  waiting for transfers between devices  33.6 us (24%)
  starting transfers between devices  29.9 us (22%)
  local copies, waits for them, and re-layouts  16.2 us (12%)
  other arithmetic  10.3 us (7%)
  matrix products  8.77 us (6%)
  between operations  1.73 us (1%)
    psum x2, blocking collectives, two_products(): lax.psum(lax.psum((jnp.sum(residual * residual, axis=(0, 1, 2)), jnp.sum(...  25.3 us
    ppermute x12, starting transfers between devices, from_behind(): return lax.ppermute(block, axis, route)  18.1 us
    ppermute x12, waiting for transfers between devices, from_behind(): return lax.ppermute(block, axis, route)  18 us
    ppermute x2, waiting for transfers between devices, with_halo(): after = lax.ppermute(initial, axis, down)  13.2 us
    psum x2, blocking collectives, two_products(): lax.psum((jnp.sum(residual * residual, axis=(0, 1, 2)), jnp.sum(residual...  12 us
    ppermute x2, starting transfers between devices, with_halo(): before = lax.ppermute(last, axis, up)  9.21 us
    unnamed x42, local copies, waits for them, and re-layouts  5.93 us
    dot_general x2, matrix products, spatial(): jnp.einsum('nik,hnkp->hnip', near_stiffness, nearby, precision=lax.Precis...  5.2 us
  transfers between devices with their start and end apart: 16, of which 8 were waited for; matrix products, arithmetic and copies ran while one was open for 6% of the time, Pallas kernels for 0%

profile of v1, /device:TPU:0, one launch (start us, length us, event | category | flops | bytes accessed | tf_op | source)
XLA Modules:
  0.0 137.7 jit_solution(15012892423534685494)
XLA Ops:
  0.6 0.0 copy-start
  0.6 0.9 copy.19
  1.5 0.1 reshape_squeeze.8
  1.6 0.5 copy-done.8
  2.1 0.7 fusion.15
  2.9 0.8 copy.18
  3.6 0.1 reshape.135
  3.7 0.0 copy-start.4
  3.8 1.7 %gather_fusion.1 = f32[24,64,128]{2,1,0:T(8,128)S(1)} fusion(f32[16,64,128]{2,1,0:T(8,128)} %bitcast.116, s32[1024]{0:T(1024)S(1)} %get-tuple-element.34), kind=kCustom, calls=%fused_computation.1.clone | custom fusion | bytes 1572960 | tf_op jit(solution)/shard_map/jit(_take)/gather | solution.py:38
  5.5 0.0 copy-start.1
  5.5 0.1 bitcast_select_fusion.3
  5.6 0.1 broadcast_multiply_fusion.1
  5.7 0.8 slice_bitcast_fusion.6
  6.5 2.5 %collective-permute-start.5 = (f32[1,4,64,128]{3,2,1,0:T(8,128)S(1)}, f32[1,4,64,128]{3,2,1,0:T(8,128)}, u32[]{:S(2)}, u32[]{:S(2)}) collective-permute-start(f32[1,4,64,128]{3,2,1,0:T(8,128)S(1)} %get-tuple-element.26), channel_id=1, source_target_pairs={{9,0},{12,1},{13,4},{0,5},{1,8},{4,9},{5,12},{8,13},{11,2},{14,3},... | collective-permute-start | bytes 393224 | tf_op jit(solution)/shard_map/ppermute | solution.py:12
  9.0 1.0 collective-permute-start.4
  10.0 2.2 %collective-permute-start.3 = (f32[1,4,64,128]{3,2,1,0:T(8,128)}, f32[1,4,64,128]{3,2,1,0:T(8,128)}, u32[]{:S(2)}, u32[]{:S(2)}) collective-permute-start(f32[1,4,64,128]{3,2,1,0:T(8,128)} %get-tuple-element.28), channel_id=1, source_target_pairs={{12,0},{13,1},{0,4},{1,5},{4,8},{5,9},{8,12},{9,13},{14,2},{15,3},... | collective-permute-start | bytes 393224 | tf_op jit(solution)/shard_map/ppermute | solution.py:12
  12.2 2.0 %collective-permute-start.2 = (f32[1,4,64,128]{3,2,1,0:T(8,128)}, f32[1,4,64,128]{3,2,1,0:T(8,128)}, u32[]{:S(2)}, u32[]{:S(2)}) collective-permute-start(f32[1,4,64,128]{3,2,1,0:T(8,128)} %get-tuple-element.29), channel_id=1, source_target_pairs={{4,0},{5,1},{8,4},{9,5},{12,8},{13,9},{0,12},{1,13},{6,2},{7,3},{1... | collective-permute-start | bytes 393224 | tf_op jit(solution)/shard_map/ppermute | solution.py:12
  14.2 0.7 collective-permute-start
  14.9 0.2 reshape_squeeze.9
  15.1 2.4 %gather_fusion = f32[96,64,128]{2,1,0:T(8,128)} fusion(f32[16,64,128]{2,1,0:T(8,128)S(1)} %bitcast.117, s32[1024]{0:T(1024)S(1)} %get-tuple-element.35), kind=kCustom, calls=%fused_computation.clone | custom fusion | bytes 6291840 | tf_op jit(solution)/shard_map/jit(_take)/gather | solution.py:46
  17.5 2.2 %bitcast_select_fusion.1 = f32[1,96,64,128]{3,2,1,0:T(8,128)S(1)} fusion(f32[96,64,128]{2,1,0:T(8,128)} %gather_fusion, pred[96]{0:T(512)(128)(4,1)S(1)} %compare_and_fusion.1), kind=kLoop, calls=%fused_computation.5 | loop fusion | flops 786432 | bytes 6291552 | tf_op jit(solution)/shard_map/jit(_take)/select_n | solution.py:46
  19.8 3.2 %collective-permute-done = f32[1,4,64,128]{3,2,1,0:T(8,128)} collective-permute-done((f32[1,4,64,128]{3,2,1,0:T(8,128)}, f32[1,4,64,128]{3,2,1,0:T(8,128)}, u32[]{:S(2)}, u32[]{:S(2)}) %collective-permute-start) | collective-permute-done | bytes 131104 | tf_op jit(solution)/shard_map/ppermute | solution.py:12
  22.9 1.4 collective-permute-start.1
  24.3 0.9 bitcast_dynamic-update-slice_fusion.11
  25.2 4.2 %collective-permute-done.1 = f32[1,4,64,128]{3,2,1,0:T(8,128)S(1)} collective-permute-done((f32[1,4,64,128]{3,2,1,0:T(8,128)S(1)}, f32[1,4,64,128]{3,2,1,0:T(8,128)S(1)}, u32[]{:S(2)}, u32[]{:S(2)}) %collective-permute-start.1) | collective-permute-done | bytes 131104 | tf_op jit(solution)/shard_map/ppermute | solution.py:12
  29.4 0.9 bitcast_dynamic-update-slice_fusion.9
  30.4 0.9 bitcast_dynamic-update-slice_fusion.8
  31.3 0.9 bitcast_dynamic-update-slice_fusion.7
  32.2 0.9 bitcast_dynamic-update-slice_fusion.6
  33.1 0.9 convolution_bitcast_fusion.1
  34.1 0.9 fusion.6
  34.9 2.6 %fusion.1 = f32[1,16,64,128]{3,2,1,0:T(8,128)S(1)} fusion(f32[16,384,128]{2,1,0:T(8,128)S(1)} %bitcast.121, f32[16,64,384]{2,1,0:T(8,128)S(1)} %copy-done, f32[64,128,16]{1,2,0:T(8,128)S(1)} %fusion.6, f32[1,16,64,128]{3,2,1,0:T(8,128)S(1)} %copy-done.1, f32[16,64]{1,0:T(8,128)S(1)} %broadcast_add_fusion), kind=kOutput, calls=%fused_computation.11 | convolution fusion | flops 604372992 | bytes 6295552 | tf_op jit(solution)/shard_map/nik,hnkp->hnip/dot_general | solution.py:50
  37.5 1.3 collective-permute-start.7
  38.8 4.6 %collective-permute-start.6 = (f32[1,16,64,128]{3,2,1,0:T(8,128)S(1)}, f32[1,16,64,128]{3,2,1,0:T(8,128)S(1)}, u32[]{:S(2)}, u32[]{:S(2)}) collective-permute-start(f32[1,16,64,128]{3,2,1,0:T(8,128)S(1)} %fusion.1), channel_id=1, source_target_pairs={{0,2},{1,3},{4,6},{5,7},{8,10},{9,11},{12,14},{13,15},{16,18},{17,... | collective-permute-start | bytes 1572872 | tf_op jit(solution)/shard_map/ppermute | solution.py:22
  44.1 6.0 %collective-permute-done.7 = f32[1,16,64,128]{3,2,1,0:T(8,128)S(1)} collective-permute-done((f32[1,16,64,128]{3,2,1,0:T(8,128)S(1)}, f32[1,16,64,128]{3,2,1,0:T(8,128)S(1)}, u32[]{:S(2)}, u32[]{:S(2)}) %collective-permute-start.7) | collective-permute-done | bytes 524320 | tf_op jit(solution)/shard_map/ppermute | solution.py:23
  50.1 1.2 collective-permute-done.6
  51.3 1.0 multiply_reduce_fusion.2
  52.3 6.0 %all-reduce.1 = (f32[128]{0:T(128)S(1)}, f32[128]{0:T(128)S(1)}) all-reduce(f32[128]{0:T(128)S(1)} %get-tuple-element.7, f32[128]{0:T(128)S(1)} %get-tuple-element.6), channel_id=1, replica_groups=mesh['grp'=2,'mesh'=4,'tm'=2,'rep'=2] {'tm','rep'}, use_global_device_ids=true, to_apply=%region_1.2 | all-reduce | flops 256 | bytes 2048 | tf_op jit(solution)/shard_map/psum | solution.py:95
  58.3 13.5 %all-reduce.3 = (f32[128]{0:T(128)S(1)}, f32[128]{0:T(128)S(1)}) all-reduce(f32[128]{0:T(128)S(1)} %get-tuple-element.10, f32[128]{0:T(128)S(1)} %get-tuple-element.11), channel_id=1, replica_groups=mesh['grp'=2,'mesh'=4,'tm'=2,'rep'=2] {'mesh'}, use_global_device_ids=true, to_apply=%region_2.3 | all-reduce | flops 256 | bytes 2048 | tf_op jit(solution)/shard_map/psum | solution.py:94
  71.8 1.1 multiply_subtract_fusion.2
  72.9 1.6 %gather_fusion.3 = f32[24,64,128]{2,1,0:T(8,128)} fusion(f32[16,64,128]{2,1,0:T(8,128)S(1)} %bitcast.118, s32[1024]{0:T(1024)} %copy-done.7), kind=kCustom, calls=%fused_computation.3.clone | custom fusion | bytes 1572960 | tf_op jit(solution)/shard_map/jit(_take)/gather | solution.py:38
  74.6 2.4 %gather_fusion.2 = f32[96,64,128]{2,1,0:T(8,128)} fusion(f32[16,64,128]{2,1,0:T(8,128)S(1)} %bitcast.119, s32[1024]{0:T(1024)S(1)} %get-tuple-element.35), kind=kCustom, calls=%fused_computation.2.clone | custom fusion | bytes 6291840 | tf_op jit(solution)/shard_map/jit(_take)/gather | solution.py:46
  77.0 1.4 %bitcast_select_fusion.2 = f32[1,24,64,128]{3,2,1,0:T(8,128)S(1)} fusion(f32[24,64,128]{2,1,0:T(8,128)} %gather_fusion.3, pred[24]{0:T(512)(128)(4,1)S(1)} %copy-done.12), kind=kLoop, calls=%fused_computation.14 | loop fusion | flops 196608 | bytes 1572888 | tf_op jit(solution)/shard_map/jit(_take)/select_n | solution.py:38
  78.4 0.1 broadcast_multiply_fusion
  78.5 0.1 slice_bitcast_fusion
  78.5 0.1 collective-permute-start.13
  78.6 2.6 %collective-permute-start.12 = (f32[1,4,64,128]{3,2,1,0:T(8,128)S(1)}, f32[1,4,64,128]{3,2,1,0:T(8,128)S(1)}, u32[]{:S(2)}, u32[]{:S(2)}) collective-permute-start(f32[1,4,64,128]{3,2,1,0:T(8,128)S(1)} %get-tuple-element.21), channel_id=1, source_target_pairs={{5,0},{8,1},{9,4},{12,5},{13,8},{0,9},{1,12},{4,13},{7,2},{10,3},{... | collective-permute-start | bytes 393224 | tf_op jit(solution)/shard_map/ppermute | solution.py:12
  81.3 3.8 %collective-permute-start.10 = (f32[1,4,64,128]{3,2,1,0:T(8,128)S(1)}, f32[1,4,64,128]{3,2,1,0:T(8,128)S(1)}, u32[]{:S(2)}, u32[]{:S(2)}) collective-permute-start(f32[1,4,64,128]{3,2,1,0:T(8,128)S(1)} %get-tuple-element.23), channel_id=1, source_target_pairs={{4,0},{5,1},{8,4},{9,5},{12,8},{13,9},{0,12},{1,13},{6,2},{7,3},{1... | collective-permute-start | bytes 393224 | tf_op jit(solution)/shard_map/ppermute | solution.py:12
  85.1 0.3 bitcast_select_fusion
  85.4 6.1 %collective-permute-done.8 = f32[1,4,64,128]{3,2,1,0:T(8,128)S(1)} collective-permute-done((f32[1,4,64,128]{3,2,1,0:T(8,128)S(1)}, f32[1,4,64,128]{3,2,1,0:T(8,128)S(1)}, u32[]{:S(2)}, u32[]{:S(2)}) %collective-permute-start.8) | collective-permute-done | bytes 131104 | tf_op jit(solution)/shard_map/ppermute | solution.py:12
  91.4 1.8 %collective-permute-start.9 = (f32[1,4,64,128]{3,2,1,0:T(8,128)S(1)}, f32[1,4,64,128]{3,2,1,0:T(8,128)S(1)}, u32[]{:S(2)}, u32[]{:S(2)}) collective-permute-start(f32[1,4,64,128]{3,2,1,0:T(8,128)S(1)} %get-tuple-element.24), channel_id=1, source_target_pairs={{13,0},{0,1},{1,4},{4,5},{5,8},{8,9},{9,12},{12,13},{15,2},{2,3},{... | collective-permute-start | bytes 393224 | tf_op jit(solution)/shard_map/ppermute | solution.py:12
  93.3 4.6 %collective-permute-done.9 = f32[1,4,64,128]{3,2,1,0:T(8,128)S(1)} collective-permute-done((f32[1,4,64,128]{3,2,1,0:T(8,128)S(1)}, f32[1,4,64,128]{3,2,1,0:T(8,128)S(1)}, u32[]{:S(2)}, u32[]{:S(2)}) %collective-permute-start.9) | collective-permute-done | bytes 131104 | tf_op jit(solution)/shard_map/ppermute | solution.py:12
  98.0 0.9 convolution_bitcast_fusion
  98.9 0.9 fusion.4
  99.8 0.0 copy-start.3
  99.8 2.6 %fusion.3 = f32[1,16,64,128]{3,2,1,0:T(8,128)S(1)} fusion(f32[16,384,128]{2,1,0:T(8,128)S(1)} %bitcast.120, f32[16,64,384]{2,1,0:T(8,128)S(1)} %copy-done, f32[64,128,16]{1,2,0:T(8,128)S(1)} %fusion.4, f32[1,16,64,128]{3,2,1,0:T(8,128)S(1)} %multiply_subtract_fusion.2, f32[16,64]{1,0:T(8,128)S(1)} %broadcast_add_fusion), kind=kOutput, calls=%fused_computation.13 | convolution fusion | flops 604372992 | bytes 6295552 | tf_op jit(solution)/shard_map/nik,hnkp->hnip/dot_general | solution.py:50
  102.4 1.3 collective-permute-start.15
  103.7 4.6 %collective-permute-start.14 = (f32[1,16,64,128]{3,2,1,0:T(8,128)S(1)}, f32[1,16,64,128]{3,2,1,0:T(8,128)S(1)}, u32[]{:S(2)}, u32[]{:S(2)}) collective-permute-start(f32[1,16,64,128]{3,2,1,0:T(8,128)S(1)} %fusion.3), channel_id=1, source_target_pairs={{0,2},{1,3},{4,6},{5,7},{8,10},{9,11},{12,14},{13,15},{16,18},{17,... | collective-permute-start | bytes 1572872 | tf_op jit(solution)/shard_map/ppermute | solution.py:22
  108.3 7.2 %collective-permute-done.15 = f32[1,16,64,128]{3,2,1,0:T(8,128)S(1)} collective-permute-done((f32[1,16,64,128]{3,2,1,0:T(8,128)S(1)}, f32[1,16,64,128]{3,2,1,0:T(8,128)S(1)}, u32[]{:S(2)}, u32[]{:S(2)}) %collective-permute-start.15) | collective-permute-done | bytes 524320 | tf_op jit(solution)/shard_map/ppermute | solution.py:23
  115.5 1.2 collective-permute-done.14
  116.7 1.0 multiply_reduce_fusion
  117.7 6.0 %all-reduce = (f32[128]{0:T(128)S(1)}, f32[128]{0:T(128)S(1)}) all-reduce(f32[128]{0:T(128)S(1)} %get-tuple-element.5, f32[128]{0:T(128)S(1)} %get-tuple-element.4), channel_id=1, replica_groups=mesh['grp'=2,'mesh'=4,'tm'=2,'rep'=2] {'tm','rep'}, use_global_device_ids=true, to_apply=%region_7.10 | all-reduce | flops 256 | bytes 2048 | tf_op jit(solution)/shard_map/psum | solution.py:95
  123.7 11.8 %all-reduce.2 = (f32[128]{0:T(128)S(1)}, f32[128]{0:T(128)S(1)}) all-reduce(f32[128]{0:T(128)S(1)} %get-tuple-element.8, f32[128]{0:T(128)S(1)} %get-tuple-element.9), channel_id=1, replica_groups=mesh['grp'=2,'mesh'=4,'tm'=2,'rep'=2] {'mesh'}, use_global_device_ids=true, to_apply=%region_8.11 | all-reduce | flops 256 | bytes 2048 | tf_op jit(solution)/shard_map/psum | solution.py:94
  135.5 2.2 %multiply_subtract_fusion = (f32[1,16,64,128]{3,2,1,0:T(8,128)}, f32[1,16,64,128]{3,2,1,0:T(8,128)}) fusion(f32[1,16,64,128]{3,2,1,0:T(8,128)S(1)} %multiply_subtract_fusion.2, f32[1,16,64,128]{3,2,1,0:T(8,128)} %get-tuple-element.18, f32[1,16,64,128]{3,2,1,0:T(8,128)S(1)} %copy-done.3, f32[128]{0:T(128)S(1)} %get-tuple-element.17, ...), kind=kLoop, calls=%fused_computation.22 | loop fusion | flops 1179648 | bytes 3147264 | tf_op jit(solution)/shard_map/sub | solution.py:138
  (50 shorter events, 0.2 us)
Async XLA Ops:
  0.6 34.3 %copy-start = (f32[16,64,384]{2,1,0:T(8,128)S(1)}, f32[16,64,384]{2,1,0:T(8,128)}, u32[]{:S(2)}) copy-start(f32[16,64,384]{2,1,0:T(8,128)} %param.15) | copy-start | bytes 4718596
  1.6 0.5 copy-start.8
  1.6 4.0 %copy-start.11 = (pred[24]{0:T(512)(128)(4,1)}, pred[24]{0:T(512)(128)(4,1)S(1)}, u32[]{:S(2)}) copy-start(pred[24]{0:T(512)(128)(4,1)S(1)} %compare_and_fusion) | copy-start | bytes 76
  3.7 1.9 %copy-start.7 = (s32[1024]{0:T(1024)}, s32[1024]{0:T(1024)S(1)}, u32[]{:S(2)}) copy-start(s32[1024]{0:T(1024)S(1)} %get-tuple-element.34) | copy-start | bytes 12292
  3.7 11.2 %copy-start.4 = (f32[1,64,1536]{2,1,0:T(8,128)S(1)}, f32[1,64,1536]{2,1,0:T(8,128)}, u32[]{:S(2)}) copy-start(f32[1,64,1536]{2,1,0:T(8,128)} %param.16) | copy-start | bytes 1179652
  5.5 9.6 %copy-start.1 = (f32[1,16,64,128]{3,2,1,0:T(8,128)S(1)}, f32[1,16,64,128]{3,2,1,0:T(8,128)}, u32[]{:S(2)}) copy-start(f32[1,16,64,128]{3,2,1,0:T(8,128)} %param.12) | copy-start | bytes 1572868
  6.5 25.7 %collective-permute-start.5 = (f32[1,4,64,128]{3,2,1,0:T(8,128)S(1)}, f32[1,4,64,128]{3,2,1,0:T(8,128)}, u32[]{:S(2)}, u32[]{:S(2)}) collective-permute-start(f32[1,4,64,128]{3,2,1,0:T(8,128)S(1)} %get-tuple-element.26), channel_id=1, source_target_pairs={{9,0},{12,1},{13,4},{0,5},{1,8},{4,9},{5,12},{8,13},{11,2},{14,3},... | collective-permute-start | bytes 393224 | tf_op jit(solution)/shard_map/ppermute | solution.py:12
  9.0 22.3 %collective-permute-start.4 = (f32[1,4,64,128]{3,2,1,0:T(8,128)S(1)}, f32[1,4,64,128]{3,2,1,0:T(8,128)}, u32[]{:S(2)}, u32[]{:S(2)}) collective-permute-start(f32[1,4,64,128]{3,2,1,0:T(8,128)S(1)} %get-tuple-element.27), channel_id=1, source_target_pairs={{5,0},{8,1},{9,4},{12,5},{13,8},{0,9},{1,12},{4,13},{7,2},{10,3},{... | collective-permute-start | bytes 393224 | tf_op jit(solution)/shard_map/ppermute | solution.py:12
  10.0 20.3 %collective-permute-start.3 = (f32[1,4,64,128]{3,2,1,0:T(8,128)}, f32[1,4,64,128]{3,2,1,0:T(8,128)}, u32[]{:S(2)}, u32[]{:S(2)}) collective-permute-start(f32[1,4,64,128]{3,2,1,0:T(8,128)} %get-tuple-element.28), channel_id=1, source_target_pairs={{12,0},{13,1},{0,4},{1,5},{4,8},{5,9},{8,12},{9,13},{14,2},{15,3},... | collective-permute-start | bytes 393224 | tf_op jit(solution)/shard_map/ppermute | solution.py:12
  12.2 17.2 %collective-permute-start.2 = (f32[1,4,64,128]{3,2,1,0:T(8,128)}, f32[1,4,64,128]{3,2,1,0:T(8,128)}, u32[]{:S(2)}, u32[]{:S(2)}) collective-permute-start(f32[1,4,64,128]{3,2,1,0:T(8,128)} %get-tuple-element.29), channel_id=1, source_target_pairs={{4,0},{5,1},{8,4},{9,5},{12,8},{13,9},{0,12},{1,13},{6,2},{7,3},{1... | collective-permute-start | bytes 393224 | tf_op jit(solution)/shard_map/ppermute | solution.py:12
  14.2 8.7 %collective-permute-start = (f32[1,4,64,128]{3,2,1,0:T(8,128)}, f32[1,4,64,128]{3,2,1,0:T(8,128)}, u32[]{:S(2)}, u32[]{:S(2)}) collective-permute-start(f32[1,4,64,128]{3,2,1,0:T(8,128)} %get-tuple-element.31), channel_id=1, source_target_pairs={{1,0},{4,1},{5,4},{8,5},{9,8},{12,9},{13,12},{0,13},{3,2},{6,3},{7... | collective-permute-start | bytes 393224 | tf_op jit(solution)/shard_map/ppermute | solution.py:12
  14.9 2.6 %copy-start.13 = (pred[96]{0:T(512)(128)(4,1)}, pred[96]{0:T(512)(128)(4,1)S(1)}, u32[]{:S(2)}) copy-start(pred[96]{0:T(512)(128)(4,1)S(1)} %compare_and_fusion.1) | copy-start | bytes 292
  17.5 2.2 %copy-start.6 = (f32[16,64]{1,0:T(8,128)S(1)}, f32[16,64]{1,0:T(8,128)}, u32[]{:S(2)}) copy-start(f32[16,64]{1,0:T(8,128)} %param.13) | copy-start | bytes 12292
  17.5 5.4 %copy-start.5 = (f32[1,4,64,128]{3,2,1,0:T(8,128)S(1)}, f32[1,4,64,128]{3,2,1,0:T(8,128)}, u32[]{:S(2)}) copy-start(f32[1,4,64,128]{3,2,1,0:T(8,128)} %get-tuple-element.30) | copy-start | bytes 393220
  19.7 14.3 %copy-start.9 = (s32[24]{0:T(128)S(1)}, s32[24]{0:T(128)}, u32[]{:S(2)}) copy-start(s32[24]{0:T(128)} %copy-done.8) | copy-start | bytes 292
  22.9 6.5 %collective-permute-start.1 = (f32[1,4,64,128]{3,2,1,0:T(8,128)S(1)}, f32[1,4,64,128]{3,2,1,0:T(8,128)S(1)}, u32[]{:S(2)}, u32[]{:S(2)}) collective-permute-start(f32[1,4,64,128]{3,2,1,0:T(8,128)S(1)} %copy-done.5), channel_id=1, source_target_pairs={{13,0},{0,1},{1,4},{4,5},{5,8},{8,9},{9,12},{12,13},{15,2},{2,3},{... | collective-permute-start | bytes 393224 | tf_op jit(solution)/shard_map/ppermute | solution.py:12
  37.5 12.6 %collective-permute-start.7 = (f32[1,16,64,128]{3,2,1,0:T(8,128)S(1)}, f32[1,16,64,128]{3,2,1,0:T(8,128)S(1)}, u32[]{:S(2)}, u32[]{:S(2)}) collective-permute-start(f32[1,16,64,128]{3,2,1,0:T(8,128)S(1)} %fusion.1), channel_id=1, source_target_pairs={{2,0},{3,1},{6,4},{7,5},{10,8},{11,9},{14,12},{15,13},{18,16},{19,... | collective-permute-start | bytes 1572872 | tf_op jit(solution)/shard_map/ppermute | solution.py:23
  38.8 12.5 %collective-permute-start.6 = (f32[1,16,64,128]{3,2,1,0:T(8,128)S(1)}, f32[1,16,64,128]{3,2,1,0:T(8,128)S(1)}, u32[]{:S(2)}, u32[]{:S(2)}) collective-permute-start(f32[1,16,64,128]{3,2,1,0:T(8,128)S(1)} %fusion.1), channel_id=1, source_target_pairs={{0,2},{1,3},{4,6},{5,7},{8,10},{9,11},{12,14},{13,15},{16,18},{17,... | collective-permute-start | bytes 1572872 | tf_op jit(solution)/shard_map/ppermute | solution.py:22
  74.5 2.4 %copy-start.12 = (pred[24]{0:T(512)(128)(4,1)S(1)}, pred[24]{0:T(512)(128)(4,1)}, u32[]{:S(2)}) copy-start(pred[24]{0:T(512)(128)(4,1)} %copy-done.11) | copy-start | bytes 76
  76.9 8.1 %copy-start.2 = (f32[96,64,128]{2,1,0:T(8,128)S(1)}, f32[96,64,128]{2,1,0:T(8,128)}, u32[]{:S(2)}) copy-start(f32[96,64,128]{2,1,0:T(8,128)} %gather_fusion.2) | copy-start | bytes 9437188
  77.0 8.1 %copy-start.14 = (pred[96]{0:T(512)(128)(4,1)S(1)}, pred[96]{0:T(512)(128)(4,1)}, u32[]{:S(2)}) copy-start(pred[96]{0:T(512)(128)(4,1)} %copy-done.13) | copy-start | bytes 292
  78.5 19.4 %collective-permute-start.13 = (f32[1,4,64,128]{3,2,1,0:T(8,128)S(1)}, f32[1,4,64,128]{3,2,1,0:T(8,128)S(1)}, u32[]{:S(2)}, u32[]{:S(2)}) collective-permute-start(f32[1,4,64,128]{3,2,1,0:T(8,128)S(1)} %get-tuple-element.20), channel_id=1, source_target_pairs={{9,0},{12,1},{13,4},{0,5},{1,8},{4,9},{5,12},{8,13},{11,2},{14,3},... | collective-permute-start | bytes 393224 | tf_op jit(solution)/shard_map/ppermute | solution.py:12
  78.6 19.3 %collective-permute-start.12 = (f32[1,4,64,128]{3,2,1,0:T(8,128)S(1)}, f32[1,4,64,128]{3,2,1,0:T(8,128)S(1)}, u32[]{:S(2)}, u32[]{:S(2)}) collective-permute-start(f32[1,4,64,128]{3,2,1,0:T(8,128)S(1)} %get-tuple-element.21), channel_id=1, source_target_pairs={{5,0},{8,1},{9,4},{12,5},{13,8},{0,9},{1,12},{4,13},{7,2},{10,3},{... | collective-permute-start | bytes 393224 | tf_op jit(solution)/shard_map/ppermute | solution.py:12
  81.2 16.7 %collective-permute-start.11 = (f32[1,4,64,128]{3,2,1,0:T(8,128)S(1)}, f32[1,4,64,128]{3,2,1,0:T(8,128)S(1)}, u32[]{:S(2)}, u32[]{:S(2)}) collective-permute-start(f32[1,4,64,128]{3,2,1,0:T(8,128)S(1)} %get-tuple-element.22), channel_id=1, source_target_pairs={{12,0},{13,1},{0,4},{1,5},{4,8},{5,9},{8,12},{9,13},{14,2},{15,3},... | collective-permute-start | bytes 393224 | tf_op jit(solution)/shard_map/ppermute | solution.py:12
  81.3 16.6 %collective-permute-start.10 = (f32[1,4,64,128]{3,2,1,0:T(8,128)S(1)}, f32[1,4,64,128]{3,2,1,0:T(8,128)S(1)}, u32[]{:S(2)}, u32[]{:S(2)}) collective-permute-start(f32[1,4,64,128]{3,2,1,0:T(8,128)S(1)} %get-tuple-element.23), channel_id=1, source_target_pairs={{4,0},{5,1},{8,4},{9,5},{12,8},{13,9},{0,12},{1,13},{6,2},{7,3},{1... | collective-permute-start | bytes 393224 | tf_op jit(solution)/shard_map/ppermute | solution.py:12
  85.1 6.4 %collective-permute-start.8 = (f32[1,4,64,128]{3,2,1,0:T(8,128)S(1)}, f32[1,4,64,128]{3,2,1,0:T(8,128)S(1)}, u32[]{:S(2)}, u32[]{:S(2)}) collective-permute-start(f32[1,4,64,128]{3,2,1,0:T(8,128)S(1)} %get-tuple-element.25), channel_id=1, source_target_pairs={{1,0},{4,1},{5,4},{8,5},{9,8},{12,9},{13,12},{0,13},{3,2},{6,3},{7... | collective-permute-start | bytes 393224 | tf_op jit(solution)/shard_map/ppermute | solution.py:12
  85.4 13.6 %copy-start.10 = (s32[24]{0:T(128)S(1)}, s32[24]{0:T(128)}, u32[]{:S(2)}) copy-start(s32[24]{0:T(128)} %copy-done.8) | copy-start | bytes 292
  91.4 6.4 %collective-permute-start.9 = (f32[1,4,64,128]{3,2,1,0:T(8,128)S(1)}, f32[1,4,64,128]{3,2,1,0:T(8,128)S(1)}, u32[]{:S(2)}, u32[]{:S(2)}) collective-permute-start(f32[1,4,64,128]{3,2,1,0:T(8,128)S(1)} %get-tuple-element.24), channel_id=1, source_target_pairs={{13,0},{0,1},{1,4},{4,5},{5,8},{8,9},{9,12},{12,13},{15,2},{2,3},{... | collective-permute-start | bytes 393224 | tf_op jit(solution)/shard_map/ppermute | solution.py:12
  99.8 35.7 %copy-start.3 = (f32[1,16,64,128]{3,2,1,0:T(8,128)S(1)}, f32[1,16,64,128]{3,2,1,0:T(8,128)}, u32[]{:S(2)}) copy-start(f32[1,16,64,128]{3,2,1,0:T(8,128)} %get-tuple-element.19) | copy-start | bytes 1572868
  102.4 13.1 %collective-permute-start.15 = (f32[1,16,64,128]{3,2,1,0:T(8,128)S(1)}, f32[1,16,64,128]{3,2,1,0:T(8,128)S(1)}, u32[]{:S(2)}, u32[]{:S(2)}) collective-permute-start(f32[1,16,64,128]{3,2,1,0:T(8,128)S(1)} %fusion.3), channel_id=1, source_target_pairs={{2,0},{3,1},{6,4},{7,5},{10,8},{11,9},{14,12},{15,13},{18,16},{19,... | collective-permute-start | bytes 1572872 | tf_op jit(solution)/shard_map/ppermute | solution.py:23
  103.7 13.0 %collective-permute-start.14 = (f32[1,16,64,128]{3,2,1,0:T(8,128)S(1)}, f32[1,16,64,128]{3,2,1,0:T(8,128)S(1)}, u32[]{:S(2)}, u32[]{:S(2)}) collective-permute-start(f32[1,16,64,128]{3,2,1,0:T(8,128)S(1)} %fusion.3), channel_id=1, source_target_pairs={{0,2},{1,3},{4,6},{5,7},{8,10},{9,11},{12,14},{13,15},{16,18},{17,... | collective-permute-start | bytes 1572872 | tf_op jit(solution)/shard_map/ppermute | solution.py:22
